TPU v7x, 512 devices: a whole 4x4x16 slice. The times are simulated.
512 devices in a mesh: img: 16 (over y, z_hi, core), ref: 32 (over z_lo, x).
Axes of the slice: x: 4, y: 4, z: 16 (z_hi: 2, z_lo: 8; z = z_hi * 8 + z_lo), core: 2. Of those that a mesh axis runs over, the one named last changes fastest.
Arguments:
- images: float32 [2, 256, 32768], P(None, 'img', 'ref'), may hold values from -6 to 6
- references: float32 [2, 256, 32768], P(None, 'ref', 'img'), may hold values from -2 to 2
- precision: float32 [256], P('img'), may hold values from 0.00390625 to 0.0390625
- shifts: int32 [12, 2], replicated, may hold values from -6 to 6, as said below
- labels: int32 [256], P('ref'), may hold values from 0 to 3
- log_prior: float32 [4], replicated, may hold values from -4 to 4
Outputs:
- new_refs: float32 [2, 256, 32768], P(None, 'ref', 'img')
- class_post: float32 [256, 4], P('img')
Inputs may be any that keep to these rules, and one draw needn't show every extreme that they name: `shifts`: both ends of the range occur in every draw.
All inputs are finite; a program needn't handle non-finite values.
Results may differ from a plain program's by a relative error of at most 0.0056.
Values may be sent and summed in bfloat16 or wider, within the bound.
No kernel may reach another device: no remote copies, remote signals or barrier semaphores. Data moves between devices by JAX's collectives and lax.ppermute only.
A program may use at most 64 MiB of HBM per device.

v0:
```python
import math
import jax
import jax.numpy as jnp
from jax import lax
from jax.sharding import PartitionSpec as P

ROWS = 256
COLS = 128
SHIFTS = 12
CLASSES = 4


def phases(shifts):
    index = jnp.arange(ROWS * COLS, dtype=jnp.int32)
    freq_y = (index // COLS - ROWS // 2).astype(jnp.float32)
    freq_x = (index % COLS).astype(jnp.float32)
    shift_x = shifts[:, 0].astype(jnp.float32)[:, None]
    shift_y = shifts[:, 1].astype(jnp.float32)[:, None]
    angles = 2.0 * math.pi / ROWS * (freq_x[None, :] * shift_x + freq_y[None, :] * shift_y)
    return (jnp.cos(angles), jnp.sin(angles))


def inner_rows(left, right):
    return lax.dot_general(
        left, right, (((1,), (1,)), ((), ())), preferred_element_type=jnp.float32
    )


def inner_cols(left, right):
    return lax.dot_general(
        left, right, (((0,), (0,)), ((), ())), preferred_element_type=jnp.float32
    )


def local(images, references, precision, shifts, labels, log_prior):
    img_low = lax.all_gather(images.astype(jnp.bfloat16), "ref", axis=2, tiled=True)
    ref_low = lax.all_gather(references.astype(jnp.bfloat16), "img", axis=2, tiled=True)
    pixels = img_low.shape[2]
    img_dev = img_low.shape[1]
    ref_dev = ref_low.shape[1]
    blocks = SHIFTS // 4
    cosine, sine_part = phases(shifts)
    cos_blocks = cosine.reshape(blocks, 4, pixels)
    sin_blocks = sine_part.reshape(blocks, 4, pixels)
    ref_wide = ref_low.astype(jnp.float32)
    energy = jnp.sum(ref_wide * ref_wide, axis=(0, 2))
    onehot = (labels[:, None] == jnp.arange(CLASSES, dtype=jnp.int32)[None, :]).astype(jnp.float32)
    prior_term = jnp.sum(onehot * log_prior[None, :], axis=1)

    def cross_block(operands):
        cos_rows, sin_rows = operands
        shifted_re = (
            ref_wide[0][None] * cos_rows[:, None, :] + ref_wide[1][None] * sin_rows[:, None, :]
        ).astype(jnp.bfloat16)
        shifted_im = (
            ref_wide[1][None] * cos_rows[:, None, :] - ref_wide[0][None] * sin_rows[:, None, :]
        ).astype(jnp.bfloat16)
        return inner_rows(img_low[0], shifted_re.reshape(4 * ref_dev, pixels)) + inner_rows(
            img_low[1], shifted_im.reshape(4 * ref_dev, pixels)
        )

    cross_terms = lax.map(cross_block, (cos_blocks, sin_blocks))
    cross_terms = jnp.transpose(cross_terms, (1, 0, 2)).reshape(img_dev, SHIFTS, ref_dev)
    scores = (
        precision[:, None, None] * (cross_terms - 0.5 * energy[None, None, :])
        + prior_term[None, None, :]
    )
    local_top = jnp.max(scores, axis=(1, 2))
    top_score = lax.pmax(local_top, "ref")
    exponent = jnp.exp(scores - top_score[:, None, None])
    local_class = jnp.einsum(
        "ik,kc->ic", jnp.sum(exponent, axis=1), onehot, precision=lax.Precision.HIGHEST
    )
    row_total, class_sum = lax.psum((jnp.sum(exponent, axis=(1, 2)), local_class), "ref")
    posterior = exponent / row_total[:, None, None]
    class_post = class_sum / row_total[:, None]
    local_mass = jnp.sum(posterior, axis=(0, 1))
    post_low = posterior.astype(jnp.bfloat16).reshape(img_dev, blocks, 4 * ref_dev)
    post_low = jnp.transpose(post_low, (1, 0, 2))

    def back_block(running, operands):
        weights_blk, cos_rows, sin_rows = operands
        back_re = inner_cols(weights_blk, img_low[0]).reshape(4, ref_dev, pixels)
        back_im = inner_cols(weights_blk, img_low[1]).reshape(4, ref_dev, pixels)
        part_re = jnp.sum(back_re * cos_rows[:, None, :] - back_im * sin_rows[:, None, :], axis=0)
        part_im = jnp.sum(back_im * cos_rows[:, None, :] + back_re * sin_rows[:, None, :], axis=0)
        return (running + jnp.stack([part_re, part_im]), None)

    start_sum = jnp.zeros((2, ref_dev, pixels), jnp.float32)
    summed, unused = lax.scan(back_block, start_sum, (post_low, cos_blocks, sin_blocks))
    summed_all, ref_mass = lax.psum((summed, local_mass), "img")
    pix_block = pixels // lax.axis_size("img")
    summed_part = lax.dynamic_slice_in_dim(
        summed_all, lax.axis_index("img") * pix_block, pix_block, 2
    )
    new_refs = summed_part / (ref_mass + 1.0)[None, :, None]
    return (new_refs, class_post)


def solution(mesh):
    return jax.shard_map(
        local,
        mesh=mesh,
        in_specs=(P(None, "img", "ref"), P(None, "ref", "img"), P("img"), P(), P("ref"), P()),
        out_specs=(P(None, "ref", "img"), P("img", None)),
        check_vma=False,
    )
```

profile of v0, /device:TPU:102, one launch (start us, length us, event | category | flops | bytes accessed | tf_op | source)
XLA Modules:
  0.0 916.9 jit_solution(10611607265250826830)
XLA Ops:
  7.2 1.5 convert_element_type.63
  8.8 0.0 all-gather.5.cloned.1.call-start
  8.8 1.5 convert_element_type.69
  10.5 0.8 convert_reduce_fusion.1
  11.3 0.1 mul.203
  11.4 0.1 mul.207
  11.4 0.8 select_reduce_fusion
  12.2 0.1 add.96
  12.3 12.6 %fusion.39 = (f32[3,4,32768]{2,1,0:T(4,128)}, f32[3,4,32768]{2,1,0:T(4,128)}) fusion(f32[3,4]{1,0:T(4,128)S(1)} %mul.207, f32[32768]{0:T(1024)S(1)} %get-tuple-element.128, f32[3,4]{1,0:T(4,128)S(1)} %mul.203, f32[32768]{0:T(1024)S(1)} %get-tuple-element.127), kind=kLoop, calls=%fused_computation.44 | loop fusion | flops 1572864 | bytes 3407968 | tf_op jit(solution)/shard_map/sin | solution.py:20
  24.9 59.6 %all-gather.3.cloned.1.call-done = bf16[2,8,32768]{2,1,0:T(8,128)(2,1)} async-done(((bf16[2,8,2048]{2,1,0:T(8,128)(2,1)}), bf16[2,8,32768]{2,1,0:T(8,128)(2,1)}) %all-gather.3.cloned.1.call-update) | async-done | bytes 1048592 | tf_op jit(solution)/shard_map/all_gather | solution.py:37
  84.5 1.9 multiply_reduce_fusion
  86.4 0.1 sub.72
  86.5 2.7 convert_element_type.64
  89.2 173.8 %all-gather.5.cloned.1.call-done = bf16[2,16,32768]{2,1,0:T(8,128)(2,1)} async-done(((bf16[2,16,1024]{2,1,0:T(8,128)(2,1)}), bf16[2,16,32768]{2,1,0:T(8,128)(2,1)}) %all-gather.5.cloned.1.call-update) | async-done | bytes 2097168 | tf_op jit(solution)/shard_map/all_gather | solution.py:36
  263.0 14.6 %while.21 = (s32[]{:T(128)}, f32[3,16,32]{2,1,0:T(8,128)S(1)}, f32[2,8,32768]{2,1,0:T(8,128)}, f32[3,4,32768]{2,1,0:T(4,128)}, f32[3,4,32768]{2,1,0:T(4,128)}, /*index=5*/bf16[2,16,32768]{2,1,0:T(8,128)(2,1)}, s32[]{:T(128)}) while((s32[]{:T(128)}, f32[3,16,32]{2,1,0:T(8,128)S(1)}, f32[2,8,32768]{2,1,0:T(8,128)}, f32[3,4,32768]{2,1,0:T(4,128)}, ...), condition=%wide.region_1.2_spmd, body=%wide.region_0.1_spmd.sunk | while | flops 75497984 | bytes 31475852 | solution.py:62
  263.0 1.4 dynamic-slice_bitcast_fusion.6
  264.4 0.5 copy-done.1
  264.9 0.1 slice_bitcast_fusion.3
  265.0 1.4 copy-done.2
  266.5 0.7 fusion.69
  267.1 0.7 fusion.70
  267.9 1.4 dynamic-slice_bitcast_fusion.6
  269.3 0.5 copy-done.1
  269.8 0.1 slice_bitcast_fusion.3
  269.9 1.4 copy-done.2
  271.4 0.7 fusion.69
  272.0 0.7 fusion.70
  272.7 1.4 dynamic-slice_bitcast_fusion.6
  274.2 0.5 copy-done.1
  274.6 0.1 slice_bitcast_fusion.3
  274.8 1.4 copy-done.2
  276.2 0.7 fusion.69
  276.9 0.7 fusion.70
  277.6 0.1 copy.13
  277.7 0.1 fusion.52
  277.8 100.4 %pmax.7 = f32[16]{0:T(128)S(1)} all-reduce(f32[16]{0:T(128)S(1)} %fusion.52), channel_id=1, replica_groups=mesh['img'=16,'ref'=32] {'ref'}, use_global_device_ids=true, to_apply=%region_5.6 | all-reduce | flops 16 | bytes 128 | tf_op jit(solution)/shard_map/pmax | solution.py:69
  378.1 0.1 fusion.51
  378.3 0.1 exponential_reduce_fusion
  378.4 0.1 fusion.53
  378.5 122.7 %all-reduce = (f32[16]{0:T(128)S(1)}, f32[16,4]{0,1:T(4,128)S(1)}) all-reduce(f32[16]{0:T(128)S(1)} %fusion.51, f32[16,4]{0,1:T(4,128)S(1)} %fusion.53), channel_id=1, replica_groups=mesh['img'=16,'ref'=32] {'ref'}, use_global_device_ids=true, to_apply=%region_7.8 | all-reduce | flops 80 | bytes 640 | tf_op jit(solution)/shard_map/psum | solution.py:74
  501.2 0.1 divide_convert_fusion
  501.3 25.5 %while.22 = (s32[]{:T(128)}, f32[2,8,32768]{2,1,0:T(8,128)S(1)}, bf16[3,16,32]{1,2,0:T(8,128)(2,1)S(1)}, bf16[2,16,32768]{2,1,0:T(8,128)(2,1)}, f32[3,4,32768]{2...) while((s32[]{:T(128)}, f32[2,8,32768]{2,1,0:T(8,128)S(1)}, ...), condition=%wide.region_11.12_spmd.clone, body=%wide.region_8.11_spmd.clone.sunk | while | flops 76546048 | bytes 30425728 | solution.py:90
  501.3 1.9 fusion.73
  503.2 1.4 dynamic-slice_bitcast_fusion.7
  504.6 0.5 copy-done.3
  505.1 2.8 subtract_reduce_fusion.2
  507.9 1.8 maximum_add_fusion.2
  509.8 1.9 fusion.73
  511.7 1.4 dynamic-slice_bitcast_fusion.7
  513.1 0.5 copy-done.3
  513.6 2.8 subtract_reduce_fusion.2
  516.4 1.8 maximum_add_fusion.2
  518.2 1.9 fusion.73
  520.2 1.4 dynamic-slice_bitcast_fusion.7
  521.6 0.5 copy-done.3
  522.1 2.8 subtract_reduce_fusion.2
  524.9 1.8 maximum_add_fusion.2
  526.7 1.3 copy-done
  528.1 0.2 divide_reduce_fusion
  528.2 0.1 reduce_sum.74
  528.3 62.1 %psum.30 = f32[8]{0:T(128)S(1)} all-reduce(f32[8]{0:T(128)S(1)} %reduce_sum.75), channel_id=1, replica_groups=mesh['img'=16,'ref'=32] {'img'}, use_global_device_ids=true, to_apply=%region_15.16 | all-reduce | flops 8 | bytes 64 | tf_op jit(solution)/shard_map/psum | solution.py:91
  590.4 0.6 broadcast_divide_fusion
  591.0 317.7 %all-reduce.3.cloned.1.call-done = f32[2,8,32768]{2,1,0:T(8,128)} async-done(((f32[2,8,32768]{2,1,0:T(8,128)}), f32[2,8,32768]{2,1,0:T(8,128)}) %all-reduce.3.cloned.1.call-update) | async-done | bytes 2097168 | tf_op jit(solution)/shard_map/psum | solution.py:91
  908.7 1.6 dynamic-slice_divide_fusion
  (27 shorter events, 0.2 us)
Async XLA Ops:
  7.2 77.4 %all-gather.3.cloned.1.call-start = ((), (), s32[]{:S(2)}) async-start(), calls=%async_computation | async-start | bytes 1114112 | tf_op jit(solution)/shard_map/all_gather | solution.py:37
  8.8 254.2 %all-gather.5.cloned.1.call-start = ((), (), s32[]{:S(2)}) async-start(), calls=%async_computation.1 | async-start | bytes 2162688 | tf_op jit(solution)/shard_map/all_gather | solution.py:36
  10.4 898.3 %all-reduce.3.cloned.1.call-start = ((), (), s32[]{:S(2)}) async-start(), calls=%async_computation.2 | async-start | bytes 4194304 | tf_op jit(solution)/shard_map/psum | solution.py:91
  262.9 14.7 %copy-start.4 = (f32[16]{0:T(128)S(1)}, f32[16]{0:T(128)}, u32[]{:S(2)}) copy-start(f32[16]{0:T(128)} %param.12) | copy-start | bytes 196
  262.9 115.4 %copy-start.5 = (s32[8]{0:T(128)S(1)}, s32[8]{0:T(128)}, u32[]{:S(2)}) copy-start(s32[8]{0:T(128)} %param.14) | copy-start | bytes 100
  263.0 1.9 copy-start.1
  264.9 1.6 copy-start.2
  267.9 1.9 copy-start.1
  269.8 1.6 copy-start.2
  272.7 1.9 copy-start.1
  274.6 1.6 copy-start.2
  503.2 1.9 copy-start.3
  511.7 1.9 copy-start.3
  520.2 1.9 copy-start.3
  526.7 1.3 copy-start
Sparse Core Ops, SparseCore 0:
  11.9 72.5 all-gather.2
  86.6 176.2 all-gather.4
  528.2 380.4 all-reduce.2
where the time goes:
time: 918 us; the launch traced here: 917 us
  waiting for transfers between devices  551 us (60%)
  blocking collectives  285 us (31%)
  other arithmetic  30.1 us (3%)
  matrix products  18.4 us (2%)
  local copies, waits for them, and re-layouts  18 us (2%)
  between operations  13.8 us (2%)
    psum x1, waiting for transfers between devices, local(): summed_all, ref_mass = lax.psum((summed, local_mass), 'img')  318 us
    all_gather x1, waiting for transfers between devices, local(): lax.all_gather(images.astype(jnp.bfloat16), 'ref', axis=2, tiled=True)  174 us
    psum x1, blocking collectives, local(): lax.psum((jnp.sum(exponent, axis=(1, 2)), local_class), 'ref')  123 us
    pmax x1, blocking collectives, local(): top_score = lax.pmax(local_top, 'ref')  100 us
    psum x1, blocking collectives, local(): summed_all, ref_mass = lax.psum((summed, local_mass), 'img')  62.1 us
    all_gather x1, waiting for transfers between devices, local(): lax.all_gather(references.astype(jnp.bfloat16), 'img', axis=2, tiled=True)  59.6 us
  transfers between devices with their start and end apart: 3, of which 3 were waited for; matrix products, arithmetic and copies ran while one was open for 2% of the time, Pallas kernels for 0%

commit v1 on v0

--- a/solution.py
+++ b/solution.py
@@ -33,7 +33,12 @@
 
 
 def local(images, references, precision, shifts, labels, log_prior):
-    img_low = lax.all_gather(images.astype(jnp.bfloat16), "ref", axis=2, tiled=True)
+    img_low = jnp.concatenate(
+        lax.all_to_all(
+            jnp.stack(lax.axis_size("ref") * [images.astype(jnp.bfloat16)], 0), "ref", 0, 0
+        ),
+        2,
+    )
     ref_low = lax.all_gather(references.astype(jnp.bfloat16), "img", axis=2, tiled=True)
     pixels = img_low.shape[2]
     img_dev = img_low.shape[1]

time: 918 us -> 746 us (0.81)
  waiting for transfers between devices: 551 us -> 408 us
  blocking collectives: 285 us -> 239 us
  starting transfers between devices: 0.12 us -> 14.5 us
    all_gather x1 -> x0, waiting for transfers between devices: 174 us -> none  [local(): lax.all_gather(images.astype(jnp.bfloat16), 'ref', axis=2, tiled=True)]
    pmax x1, blocking collectives: 100 us -> 71.2 us  [local(): top_score = lax.pmax(local_top, 'ref')]
    all_gather x1, waiting for transfers between devices: 59.6 us -> 77 us  [local(): lax.all_gather(references.astype(jnp.bfloat16), 'img', axis=2, tiled=True)]
    psum x1, blocking collectives: 123 us -> 106 us  [local(): lax.psum((jnp.sum(exponent, axis=(1, 2)), local_class), 'ref')]
    all_to_all x0 -> x1, starting transfers between devices: none -> 14.4 us  [local(): lax.all_to_all(jnp.stack(lax.axis_size('ref') * [images.astype(jnp.bfloat...]
  transfers between devices with their start and end apart: 3 -> 3, of which waited for: 3 -> 3; matrix products, arithmetic and copies ran while one was open for 2% -> 3% of each run, Pallas kernels for 0% -> 0%
where the time goes in v1:
time: 746 us; the launch traced here: 745 us
  waiting for transfers between devices  408 us (55%)
  blocking collectives  239 us (32%)
  other arithmetic  27.1 us (4%)
  local copies, waits for them, and re-layouts  22.7 us (3%)
  matrix products  18.4 us (2%)
  starting transfers between devices  14.5 us (2%)
  between operations  14.2 us (2%)
    psum x1, waiting for transfers between devices, local(): summed_all, ref_mass = lax.psum((summed, local_mass), 'img')  323 us
    psum x1, blocking collectives, local(): lax.psum((jnp.sum(exponent, axis=(1, 2)), local_class), 'ref')  106 us
    all_gather x1, waiting for transfers between devices, local(): lax.all_gather(references.astype(jnp.bfloat16), 'img', axis=2, tiled=True)  77 us
    pmax x1, blocking collectives, local(): top_score = lax.pmax(local_top, 'ref')  71.2 us
    psum x1, blocking collectives, local(): summed_all, ref_mass = lax.psum((summed, local_mass), 'img')  62 us
  transfers between devices with their start and end apart: 3, of which 3 were waited for; matrix products, arithmetic and copies ran while one was open for 3% of the time, Pallas kernels for 0%

profile of v1, /device:TPU:102, one launch (start us, length us, event | category | flops | bytes accessed | tf_op | source)
XLA Modules:
  0.0 744.8 jit_solution(9368254111765697503)
XLA Ops:
  7.2 0.9 convert_element_type.69
  8.1 1.6 stack.8
  9.7 14.4 %all-to-all-start = ((bf16[32,2,16,1024]{3,2,1,0:T(8,128)(2,1)}), bf16[32,2,16,1024]{3,2,1,0:T(8,128)(2,1)}, u32[]{:S(2)}, u32[]{:S(2)}) async-start(bf16[32,2,16,1024]{3,2,1,0:T(8,128)(2,1)} %stack.8), calls=%async_computation | async-start | bytes 4194304 | tf_op jit(solution)/shard_map/all_to_all | solution.py:37
  24.2 0.6 convert_element_type.63
  25.0 0.1 mul.203
  25.1 0.1 mul.207
  25.2 12.7 %fusion.39 = (f32[3,4,32768]{2,1,0:T(4,128)}, f32[3,4,32768]{2,1,0:T(4,128)}) fusion(f32[3,4]{1,0:T(4,128)S(1)} %mul.207, f32[32768]{0:T(1024)S(1)} %get-tuple-element.128, f32[3,4]{1,0:T(4,128)S(1)} %mul.203, f32[32768]{0:T(1024)S(1)} %get-tuple-element.127), kind=kLoop, calls=%fused_computation.44 | loop fusion | flops 1572864 | bytes 3407968 | tf_op jit(solution)/shard_map/sin | solution.py:20
  37.9 0.1 select_reduce_fusion
  38.0 0.1 add.96
  38.0 77.0 %all-gather.2.cloned.1.call-done = bf16[2,8,32768]{2,1,0:T(8,128)(2,1)} async-done(((bf16[2,8,2048]{2,1,0:T(8,128)(2,1)}), bf16[2,8,32768]{2,1,0:T(8,128)(2,1)}) %all-gather.2.cloned.1.call-update) | async-done | bytes 1048592 | tf_op jit(solution)/shard_map/all_gather | solution.py:42
  115.0 1.9 multiply_reduce_fusion
  116.9 0.1 sub.72
  117.0 2.7 convert_element_type.64
  119.7 8.6 %all-to-all-done = bf16[32,2,16,1024]{3,2,1,0:T(8,128)(2,1)} async-done(((bf16[32,2,16,1024]{3,2,1,0:T(8,128)(2,1)}), bf16[32,2,16,1024]{3,2,1,0:T(8,128)(2,1)}, u32[]{:S(2)}, u32[]{:S(2)}) %all-to-all-start) | async-done | bytes 2097184 | tf_op jit(solution)/shard_map/all_to_all | solution.py:37
  128.3 3.2 copy.19
  131.4 14.6 %while.21 = (s32[]{:T(128)}, f32[3,16,32]{2,1,0:T(8,128)S(1)}, f32[2,8,32768]{2,1,0:T(8,128)}, f32[3,4,32768]{2,1,0:T(4,128)}, f32[3,4,32768]{2,1,0:T(4,128)}, /*index=5*/bf16[2,16,32768]{2,1,0:T(8,128)(2,1)}, s32[]{:T(128)}) while((s32[]{:T(128)}, f32[3,16,32]{2,1,0:T(8,128)S(1)}, f32[2,8,32768]{2,1,0:T(8,128)}, f32[3,4,32768]{2,1,0:T(4,128)}, ...), condition=%wide.region_1.2_spmd, body=%wide.region_0.1_spmd.sunk | while | flops 75497984 | bytes 31475852 | solution.py:67
  131.4 1.4 dynamic-slice_bitcast_fusion.6
  132.9 0.5 copy-done.1
  133.4 0.1 slice_bitcast_fusion.3
  133.5 1.4 copy-done.2
  135.0 0.7 fusion.69
  135.6 0.7 fusion.70
  136.3 1.4 dynamic-slice_bitcast_fusion.6
  137.8 0.5 copy-done.1
  138.2 0.1 slice_bitcast_fusion.3
  138.4 1.4 copy-done.2
  139.8 0.7 fusion.69
  140.5 0.7 fusion.70
  141.2 1.4 dynamic-slice_bitcast_fusion.6
  142.6 0.5 copy-done.1
  143.1 0.1 slice_bitcast_fusion.3
  143.3 1.4 copy-done.2
  144.7 0.7 fusion.69
  145.4 0.7 fusion.70
  146.2 0.1 fusion.52
  146.3 71.2 %pmax.7 = f32[16]{0:T(128)S(1)} all-reduce(f32[16]{0:T(128)S(1)} %fusion.52), channel_id=1, replica_groups=mesh['img'=16,'ref'=32] {'ref'}, use_global_device_ids=true, to_apply=%region_5.6 | all-reduce | flops 16 | bytes 128 | tf_op jit(solution)/shard_map/pmax | solution.py:74
  217.5 0.1 fusion.51
  217.6 0.1 exponential_reduce_fusion
  217.7 0.1 fusion.53
  217.8 106.1 %all-reduce = (f32[16]{0:T(128)S(1)}, f32[16,4]{0,1:T(4,128)S(1)}) all-reduce(f32[16]{0:T(128)S(1)} %fusion.51, f32[16,4]{0,1:T(4,128)S(1)} %fusion.53), channel_id=1, replica_groups=mesh['img'=16,'ref'=32] {'ref'}, use_global_device_ids=true, to_apply=%region_7.8 | all-reduce | flops 80 | bytes 640 | tf_op jit(solution)/shard_map/psum | solution.py:79
  323.9 0.1 divide_convert_fusion
  323.9 25.5 %while.22 = (s32[]{:T(128)}, f32[2,8,32768]{2,1,0:T(8,128)S(1)}, bf16[3,16,32]{1,2,0:T(8,128)(2,1)S(1)}, bf16[2,16,32768]{2,1,0:T(8,128)(2,1)}, f32[3,4,32768]{2...) while((s32[]{:T(128)}, f32[2,8,32768]{2,1,0:T(8,128)S(1)}, ...), condition=%wide.region_11.12_spmd.clone, body=%wide.region_8.11_spmd.clone.sunk | while | flops 76546048 | bytes 30425728 | solution.py:95
  324.0 1.9 fusion.73
  325.9 1.4 dynamic-slice_bitcast_fusion.7
  327.3 0.5 copy-done.3
  327.8 2.8 subtract_reduce_fusion.2
  330.6 1.8 maximum_add_fusion.2
  332.4 1.9 fusion.73
  334.4 1.4 dynamic-slice_bitcast_fusion.7
  335.8 0.5 copy-done.3
  336.3 2.8 subtract_reduce_fusion.2
  339.1 1.8 maximum_add_fusion.2
  340.9 1.9 fusion.73
  342.9 1.4 dynamic-slice_bitcast_fusion.7
  344.3 0.5 copy-done.3
  344.7 2.8 subtract_reduce_fusion.2
  347.6 1.8 maximum_add_fusion.2
  349.4 1.3 copy-done
  350.7 0.2 divide_reduce_fusion
  350.9 0.1 reduce_sum.74
  351.0 62.0 %psum.30 = f32[8]{0:T(128)S(1)} all-reduce(f32[8]{0:T(128)S(1)} %reduce_sum.75), channel_id=1, replica_groups=mesh['img'=16,'ref'=32] {'img'}, use_global_device_ids=true, to_apply=%region_15.16 | all-reduce | flops 8 | bytes 64 | tf_op jit(solution)/shard_map/psum | solution.py:96
  413.0 0.6 broadcast_divide_fusion
  413.6 322.8 %all-reduce.3.cloned.1.call-done = f32[2,8,32768]{2,1,0:T(8,128)} async-done(((f32[2,8,32768]{2,1,0:T(8,128)}), f32[2,8,32768]{2,1,0:T(8,128)}) %all-reduce.3.cloned.1.call-update) | async-done | bytes 2097168 | tf_op jit(solution)/shard_map/psum | solution.py:96
  736.4 1.6 dynamic-slice_divide_fusion
  (34 shorter events, 0.3 us)
Async XLA Ops:
  9.7 14.5 %copy-start.4 = (f32[2,8,2048]{2,1,0:T(8,128)S(1)}, f32[2,8,2048]{2,1,0:T(8,128)}, u32[]{:S(2)}) copy-start(f32[2,8,2048]{2,1,0:T(8,128)} %param.11) | copy-start | bytes 393220
  9.7 15.3 %copy-start.6 = (s32[12,2]{0,1:T(2,128)S(1)}, s32[12,2]{0,1:T(2,128)}, u32[]{:S(2)}) copy-start(s32[12,2]{0,1:T(2,128)} %param.13) | copy-start | bytes 292
  9.7 118.6 %all-to-all-start = ((bf16[32,2,16,1024]{3,2,1,0:T(8,128)(2,1)}), bf16[32,2,16,1024]{3,2,1,0:T(8,128)(2,1)}, u32[]{:S(2)}, u32[]{:S(2)}) async-start(bf16[32,2,16,1024]{3,2,1,0:T(8,128)(2,1)} %stack.8), calls=%async_computation | async-start | bytes 4194304 | tf_op jit(solution)/shard_map/all_to_all | solution.py:37
  24.2 13.7 %copy-start.7 = (s32[8]{0:T(128)S(1)}, s32[8]{0:T(128)}, u32[]{:S(2)}) copy-start(s32[8]{0:T(128)} %param.14) | copy-start | bytes 100
  24.2 13.7 %copy-start.8 = (f32[4]{0:T(128)S(1)}, f32[4]{0:T(128)}, u32[]{:S(2)}) copy-start(f32[4]{0:T(128)} %param.15) | copy-start | bytes 52
  24.2 90.8 %all-gather.2.cloned.1.call-start = ((), (), s32[]{:S(2)}) async-start(), calls=%async_computation.1 | async-start | bytes 1114112 | tf_op jit(solution)/shard_map/all_gather | solution.py:42
  24.9 711.5 %all-reduce.3.cloned.1.call-start = ((), (), s32[]{:S(2)}) async-start(), calls=%async_computation.2 | async-start | bytes 4194304 | tf_op jit(solution)/shard_map/psum | solution.py:96
  131.4 14.7 %copy-start.5 = (f32[16]{0:T(128)S(1)}, f32[16]{0:T(128)}, u32[]{:S(2)}) copy-start(f32[16]{0:T(128)} %param.12) | copy-start | bytes 196
  131.4 1.9 copy-start.1
  133.4 1.6 copy-start.2
  136.3 1.9 copy-start.1
  138.2 1.6 copy-start.2
  141.2 1.9 copy-start.1
  143.1 1.6 copy-start.2
  325.9 1.9 copy-start.3
  334.4 1.9 copy-start.3
  342.8 1.9 copy-start.3
  349.4 1.3 copy-start
Sparse Core Ops, SparseCore 0:
  28.9 86.0 all-gather.1
  350.8 385.4 all-reduce.2
